TPU v7x, 256 devices: a whole 4x4x8 slice. The times are simulated.
256 devices in a mesh: wide: 32 (over z, y), narrow: 8 (over x, core).
Axes of the slice: x: 4, y: 4, z: 8, core: 2. Of those that a mesh axis runs over, the one named last changes fastest.
Arguments:
- hidden: bfloat16 [160, 4096], P('wide', 'narrow'), may hold values from -18 to 18
- w_query: bfloat16 [4096, 4096], P('narrow', 'wide'), may hold values from -0.09375 to 0.09375
- w_keyval: bfloat16 [4096, 1024], P('narrow', 'wide'), may hold values from -0.09375 to 0.09375
- w_out: bfloat16 [4096, 4096], P('narrow', 'wide'), may hold values from -0.09375 to 0.09375
- pool: bfloat16 [16384, 16, 1024], P(('wide', 'narrow')), may hold values from -144 to 144
- page_req: int32 [16384], P(('wide', 'narrow')), may hold values from -1 to 31, as said below
- page_idx: int32 [16384], P(('wide', 'narrow')), may hold values from -1 to 511, as said below
- lengths: int32 [32], replicated, may hold values from 128 to 8192, as said below
- moves: int32 [16384, 1], P(('wide', 'narrow')), may hold values from 0 to 31; in each aligned block of 64 rows (0 to 63, 64 to 127, ...) at most 2 rows name the same one
- accepted: int32 [32], replicated, may hold values from 1 to 5
Outputs:
- attended: bfloat16 [160, 4096], P('narrow', 'wide')
- new_entries: bfloat16 [32, 5, 1024], P('wide')
- moved_pool: bfloat16 [16384, 16, 1024], P(('wide', 'narrow'))
- moved_req: int32 [16384], P(('wide', 'narrow'))
- moved_idx: int32 [16384], P(('wide', 'narrow'))
Inputs may be any that keep to these rules, and one draw needn't show every extreme that they name: Request r holds exactly ceil(lengths[r] / 16) slots, whose page numbers are 0 up to that count minus 1, each once; every other slot is free, with page_req and page_idx -1. `page_idx`: see page_req. `lengths`: each length lies either in 128 to 256 or in 6144 to 8192; exactly 16 lie in the second range. `moves`: each device sends exactly 2 of its slots to each index of wide.
All inputs are finite; a program needn't handle non-finite values.
Results may differ from a plain program's by a relative error of at most 0.03.
Values may be sent and summed in bfloat16 or wider, within the bound.
A program may use at most 128 MiB of HBM per device.

v0:
```python
import math
import jax
import jax.numpy as jnp
from jax import lax
from jax.sharding import PartitionSpec as P

HEADS = 32
KVH = 4
HD = 128
STEPS = 5
PAGE = 16
NEG_FILL = -1e30


def combine(first, second):
    peak = jnp.maximum(first[0], second[0])
    lead = jnp.exp(first[0] - peak)
    trail = jnp.exp(second[0] - peak)
    return (
        peak,
        first[1] * lead + second[1] * trail,
        first[2] * lead[..., None] + second[2] * trail[..., None],
    )


def on_device(hidden, w_query, w_keyval, w_out, pool, page_req, page_idx, lengths, moves, accepted):
    wide_count = lax.axis_size("wide")
    narrow_count = lax.axis_size("narrow")
    groups = HEADS // KVH
    scale = 1.0 / math.sqrt(HD)
    rows_all = lax.all_gather(hidden, "wide", axis=0, tiled=True)
    total_rows = rows_all.shape[0]
    req_total = total_rows // STEPS
    joined = jnp.concatenate([w_query, w_keyval], axis=1)
    query_cols = w_query.shape[1]
    picked = rows_all
    projected = lax.psum_scatter(
        jnp.dot(picked, joined, preferred_element_type=jnp.float32),
        "narrow",
        scatter_dimension=0,
        tiled=True,
    ).astype(jnp.bfloat16)
    query_rows, keyval_rows = (
        lax.all_gather(projected[:, :query_cols], "narrow", axis=0, tiled=True),
        lax.all_gather(projected[:, query_cols:], "narrow", axis=0, tiled=True),
    )
    query_full, keyval_full = (
        lax.all_gather(query_rows, "wide", axis=1, tiled=True),
        lax.all_gather(keyval_rows, "wide", axis=1, tiled=True),
    )
    query = query_full.reshape(req_total, STEPS, KVH, groups, HD)
    keyval = keyval_full.reshape(req_total, STEPS, 2, KVH, HD)
    pool_size = pool.shape[0]
    capacity = pool_size // wide_count
    dest = moves[:, 0]
    order = jnp.arange(pool_size, dtype=jnp.int32)
    rank = jnp.sum((dest[:, None] == dest[None, :]) & (order[None, :] < order[:, None]), axis=1)
    target = dest * capacity + rank
    source_of = jnp.sum(jnp.where(target[None, :] == order[:, None], order[None, :], 0), axis=1)
    moved = (
        lax.all_to_all(
            jnp.take(pool, source_of, axis=0), "wide", split_axis=0, concat_axis=0, tiled=True
        ),
        lax.all_to_all(
            jnp.take(page_req, source_of), "wide", split_axis=0, concat_axis=0, tiled=True
        ),
        lax.all_to_all(
            jnp.take(page_idx, source_of), "wide", split_axis=0, concat_axis=0, tiled=True
        ),
    )
    pages = moved[0]
    requests = moved[1]
    count = pages.shape[0]
    owners = jnp.maximum(requests, 0)
    cache = pages.reshape(count, PAGE, 2, KVH, HD)
    page_query = jnp.take(query, owners, axis=0)
    scores = (
        jnp.einsum(
            "pskgd,ptkd->pkgst", page_query, cache[:, :, 0], preferred_element_type=jnp.float32
        )
        * scale
    )
    positions = moved[2][:, None] * PAGE + jnp.arange(PAGE, dtype=jnp.int32)[None, :]
    visible = (positions < jnp.take(lengths, owners)[:, None]) & (requests >= 0)[:, None]
    visible = visible[:, None, None, None, :]
    scores = jnp.where(visible, scores, NEG_FILL)
    peaks = jnp.max(scores, axis=-1)
    weights = jnp.where(visible, jnp.exp(scores - peaks[..., None]), 0.0)
    totals = jnp.sum(weights, axis=-1)
    sums = jnp.einsum(
        "pkgst,ptkd->pkgsd",
        weights.astype(jnp.bfloat16),
        cache[:, :, 1],
        preferred_element_type=jnp.float32,
    )
    member = requests[None, :] == jnp.arange(req_total, dtype=jnp.int32)[:, None]
    req_peaks = jnp.max(jnp.where(member[:, :, None, None, None], peaks[None], NEG_FILL), axis=1)
    factor = jnp.exp(peaks - jnp.take(req_peaks, owners, axis=0))
    selector = member.astype(jnp.float32)
    req_totals = jnp.dot(
        selector, (totals * factor).reshape(count, -1), precision=lax.Precision.HIGHEST
    )
    req_sums = jnp.dot(
        selector, (sums * factor[..., None]).reshape(count, -1), precision=lax.Precision.HIGHEST
    )
    req_totals = req_totals.reshape(req_total, KVH, groups, STEPS)
    req_sums = req_sums.reshape(req_total, KVH, groups, STEPS, HD)
    row_peaks = jnp.transpose(req_peaks, (0, 3, 1, 2)).reshape(total_rows, HEADS)
    row_totals = jnp.transpose(req_totals, (0, 3, 1, 2)).reshape(total_rows, HEADS)
    row_sums = jnp.transpose(req_sums, (0, 3, 1, 2, 4)).reshape(total_rows, HEADS, HD)
    state = (row_peaks, row_totals, row_sums)
    fresh_scores = (
        jnp.einsum("rskgd,rtkd->rkgst", query, keyval[:, :, 0], preferred_element_type=jnp.float32)
        * scale
    )
    causal = jnp.arange(STEPS)[None, :] <= jnp.arange(STEPS)[:, None]
    fresh_scores = jnp.where(causal, fresh_scores, NEG_FILL)
    fresh_peaks = jnp.max(fresh_scores, axis=-1)
    fresh_weights = jnp.where(causal, jnp.exp(fresh_scores - fresh_peaks[..., None]), 0.0)
    fresh_totals = jnp.sum(fresh_weights, axis=-1)
    fresh_sums = jnp.einsum(
        "rkgst,rtkd->rskgd",
        fresh_weights.astype(jnp.bfloat16),
        keyval[:, :, 1],
        preferred_element_type=jnp.float32,
    )
    self_peaks = jnp.transpose(fresh_peaks, (0, 3, 1, 2)).reshape(total_rows, HEADS)
    self_totals = jnp.transpose(fresh_totals, (0, 3, 1, 2)).reshape(total_rows, HEADS)
    self_sums = fresh_sums.reshape(total_rows, HEADS, HD)
    head_count = HEADS // narrow_count
    first_head = lax.axis_index("narrow") * head_count
    mine_peaks = lax.dynamic_slice_in_dim(self_peaks, first_head, head_count, 1)
    mine_totals = lax.dynamic_slice_in_dim(self_totals, first_head, head_count, 1)
    mine_sums = lax.dynamic_slice_in_dim(self_sums, first_head, head_count, 1)
    peak_all = lax.pmax(state[0], ("wide", "narrow"))
    lead = jnp.exp(state[0] - peak_all)
    scaled_sums = (state[2] * lead[..., None]).reshape(total_rows, HEADS * HD)
    part_sums, part_totals = (
        lax.psum_scatter(
            scaled_sums.astype(jnp.bfloat16), "narrow", scatter_dimension=1, tiled=True
        ).astype(jnp.float32),
        lax.psum_scatter(
            (state[1] * lead).astype(jnp.bfloat16), "narrow", scatter_dimension=1, tiled=True
        ).astype(jnp.float32),
    )
    full_sums, full_totals = (
        lax.psum(part_sums.astype(jnp.bfloat16), "wide").astype(jnp.float32),
        lax.psum(part_totals.astype(jnp.bfloat16), "wide").astype(jnp.float32),
    )
    block_peaks = lax.dynamic_slice_in_dim(peak_all, first_head, head_count, 1)
    final = combine(
        (block_peaks, full_totals, full_sums.reshape(total_rows, head_count, HD)),
        (mine_peaks, mine_totals, mine_sums),
    )
    attn_block = (
        (final[2] / final[1][..., None]).reshape(total_rows, head_count * HD).astype(jnp.bfloat16)
    )
    picked = attn_block
    attended = lax.psum_scatter(
        jnp.dot(picked, w_out, preferred_element_type=jnp.float32).astype(jnp.bfloat16),
        "narrow",
        scatter_dimension=0,
        tiled=True,
    )
    local_req = hidden.shape[0] // STEPS
    first_req = lax.axis_index("wide") * local_req
    fresh_rows = lax.dynamic_slice_in_dim(
        keyval_full.reshape(req_total, STEPS, -1), first_req, local_req, 0
    )
    kept = lax.dynamic_slice_in_dim(accepted, first_req, local_req, 0)
    step_ids = jnp.arange(STEPS, dtype=jnp.int32)
    new_entries = jnp.where(
        step_ids[None, :, None] < kept[:, None, None], fresh_rows, jnp.zeros((), jnp.bfloat16)
    )
    return (attended, new_entries, moved[0], moved[1], moved[2])


def solution(mesh):
    in_specs = (
        P("wide", "narrow"),
        P("narrow", "wide"),
        P("narrow", "wide"),
        P("narrow", "wide"),
        P(("wide", "narrow"), None, None),
        P(("wide", "narrow")),
        P(("wide", "narrow")),
        P(),
        P(("wide", "narrow"), None),
        P(),
    )
    out_specs = (
        P("narrow", "wide"),
        P("wide", None, None),
        P(("wide", "narrow"), None, None),
        P(("wide", "narrow")),
        P(("wide", "narrow")),
    )
    return jax.shard_map(
        on_device, mesh=mesh, in_specs=in_specs, out_specs=out_specs, check_vma=False
    )
```

profile of v0, /device:TPU:8, one launch (start us, length us, event | category | flops | bytes accessed | tf_op | source)
XLA Modules:
  0.0 752.8 jit_solution(15309788727797275602)
XLA Ops:
  7.2 1.0 convert_reduce_fusion
  8.2 0.7 multiply_add_fusion.1
  9.0 1.4 gather_fusion.5
  10.4 1.4 gather_fusion.4
  11.9 0.7 all_to_all.17
  12.6 11.7 %all-to-all-start = ((s32[32,2,1]{1,2,0:T(1,128)}), s32[32,2,1]{1,2,0:T(1,128)S(1)}, u32[]{:S(2)}, u32[]{:S(2)}) async-start(s32[32,2,1]{1,2,0:T(1,128)} %bitcast.1), calls=%async_computation | async-start | bytes 32768 | tf_op jit(solution)/shard_map/all_to_all | solution.py:64
  24.3 0.7 all_to_all.19
  25.0 2.0 gather_fusion.1
  27.0 5.7 all-to-all-done
  32.7 5.0 all-to-all-start.1
  37.7 3.2 broadcast_select_fusion.1
  40.9 5.4 all-to-all-done.1
  46.3 5.6 all-to-all-start.2
  52.0 86.4 %all-gather = bf16[32,5,512]{2,1,0:T(8,128)(2,1)S(1)} all-gather(bf16[1,5,512]{2,1,0:T(8,128)(2,1)S(1)} %bitcast.133), channel_id=1, replica_groups=mesh['wide'=32,'narrow'=8] {'wide'}, dimensions={0}, use_global_device_ids=true | all-gather | bytes 168960 | tf_op jit(solution)/shard_map/all_gather | solution.py:31
  140.1 25.1 %all-reduce = bf16[160,160]{0,1:T(8,128)(2,1)S(1)} all-reduce(f32[160,160]{0,1:T(8,128)S(1)} %convolution_bitcast_fusion.1), channel_id=2, replica_groups=mesh['wide'=32,'narrow'=8] {'narrow'}, use_global_device_ids=true, to_apply=%region_2.0.clone | all-reduce | flops 25600 | bytes 153600
  165.4 12.8 %all-gather.1 = bf16[8,20,128]{2,1,0:T(8,128)(2,1)S(1)} all-gather(bf16[1,20,128]{2,1,0:T(8,128)(2,1)S(1)} %copy.106), channel_id=1, replica_groups=mesh['wide'=32,'narrow'=8] {'narrow'}, dimensions={0}, use_global_device_ids=true | all-gather | bytes 46080 | tf_op jit(solution)/shard_map/all_gather | solution.py:44
  178.3 0.6 reshape.290
  179.9 0.7 fusion.47
  180.9 0.7 reduce.11
  181.7 0.8 gather_fusion
  182.6 66.8 %all-gather.5.cloned.1.call-done = bf16[160,4096]{1,0:T(8,128)(2,1)} async-done(((bf16[160,128]{1,0:T(8,128)(2,1)}), bf16[160,4096]{1,0:T(8,128)(2,1)}) %all-gather.5.cloned.1.call-update) | async-done | bytes 1310736 | tf_op jit(solution)/shard_map/all_gather | solution.py:48
  249.5 1.6 copy.169
  251.1 2.4 gather_fusion.2
  253.4 4.4 reshape.221
  257.9 3.7 fusion.50
  261.5 3.5 bitcast_reduce_fusion
  265.5 1.2 copy.137
  266.7 0.7 select_reduce_fusion
  267.5 0.8 copy-done.4
  268.4 1.0 gather_fusion.3
  269.7 0.9 copy.111
  270.6 6.2 fusion.4
  276.8 1.8 copy.136
  279.7 75.1 %pmax.7 = f32[160,32]{0,1:T(8,128)S(1)} all-reduce(f32[160,32]{0,1:T(8,128)S(1)} %copy.119), channel_id=1, replica_groups=mesh['wide'=32,'narrow'=8] {'wide','narrow'}, use_global_device_ids=true, to_apply=%region_5.7 | all-reduce | flops 5120 | bytes 40960 | tf_op jit(solution)/shard_map/pmax | solution.py:135
  354.9 0.9 subtract_exponential_fusion
  355.9 1.8 copy.113
  357.6 5.5 broadcast_multiply_fusion
  363.1 5.1 copy.114
  368.2 6.7 reshape.223
  374.9 7.3 dot_general.39
  382.3 8.2 %fusion.17 = f32[32,5,4,8,128]{4,0,1,3,2:T(8,128)S(1)} fusion(f32[4,8,5,128,64]{3,2,1,0,4:T(8,128)} %dot_general.39, s32[64]{0:T(128)S(1)} %eq.48), kind=kOutput, calls=%fused_computation.30 | convolution fusion | flops 503318528 | bytes 7864576 | tf_op jit(solution)/shard_map/dot_general | solution.py:103
  390.5 3.0 copy.116
  393.5 4.0 reshape.224
  397.5 0.7 mul.96
  398.2 1.0 copy-done.3
  399.2 2.6 fusion.8
  401.9 0.7 slice_bitcast_fusion.1
  402.7 12.8 %all-gather.2 = bf16[8,20,32]{2,1,0:T(8,128)(2,1)S(1)} all-gather(bf16[1,20,32]{2,1,0:T(8,128)(2,1)S(1)} %copy.121), channel_id=1, replica_groups=mesh['wide'=32,'narrow'=8] {'narrow'}, dimensions={0}, use_global_device_ids=true | all-gather | bytes 11520 | tf_op jit(solution)/shard_map/all_gather | solution.py:45
  415.6 47.0 %all_gather.19 = bf16[160,1024]{0,1:T(8,128)(2,1)S(1)} all-gather(bf16[160,32]{0,1:T(8,128)(2,1)S(1)} %copy.155), channel_id=1, replica_groups=mesh['wide'=32,'narrow'=8] {'wide'}, dimensions={1}, use_global_device_ids=true | all-gather | bytes 337920 | tf_op jit(solution)/shard_map/all_gather | solution.py:49
  464.3 0.6 iota_compare_fusion.6
  465.0 0.7 dynamic-slice_select_fusion
  465.8 6.4 fusion.20
  472.2 2.5 copy.126
  476.0 2.3 copy.133
  478.3 0.8 convolution_bitcast_fusion
  479.1 1.8 copy.134
  481.1 23.9 %all-reduce.1 = bf16[160,32]{1,0:T(8,128)(2,1)S(1)} all-reduce(bf16[160,32]{1,0:T(8,128)(2,1)S(1)} %copy.142), channel_id=4, replica_groups=mesh['wide'=32,'narrow'=8] {'narrow'}, use_global_device_ids=true, to_apply=%region_10.12.clone | all-reduce | flops 5120 | bytes 20480
  505.2 72.1 %psum.15 = bf16[160,4]{0,1:T(4,128)(2,1)S(1)} all-reduce(bf16[160,4]{0,1:T(4,128)(2,1)S(1)} %copy.143), channel_id=1, replica_groups=mesh['wide'=32,'narrow'=8] {'wide'}, use_global_device_ids=true, to_apply=%region_11.13 | all-reduce | flops 640 | bytes 2560 | tf_op jit(solution)/shard_map/psum | solution.py:148
  577.3 1.6 reshape.226
  579.4 136.8 %all-reduce.5.cloned.1.call-done = bf16[160,4,128]{2,1,0:T(4,128)(2,1)} async-done(((bf16[160,4,128]{2,1,0:T(4,128)(2,1)}), bf16[160,4,128]{2,1,0:T(4,128)(2,1)}) %all-reduce.5.cloned.1.call-update) | async-done | bytes 163856 | tf_op jit(solution)/shard_map/psum | solution.py:147
  716.2 1.8 fusion.25
  718.2 23.9 %all-reduce.2 = bf16[160,128]{1,0:T(8,128)(2,1)S(1)} all-reduce(bf16[160,128]{1,0:T(8,128)(2,1)S(1)} %convolution_convert_fusion), channel_id=5, replica_groups=mesh['wide'=32,'narrow'=8] {'narrow'}, use_global_device_ids=true, to_apply=%region_13.15.clone | all-reduce | flops 20480 | bytes 81920
  742.2 0.6 constant_dynamic-slice_fusion.2
  742.8 3.2 copy.201
  (110 shorter events, 8.6 us)
Async XLA Ops:
  7.2 17.9 %copy-start = (bf16[64,16,1024]{2,1,0:T(8,128)(2,1)S(1)}, bf16[64,16,1024]{2,1,0:T(8,128)(2,1)}, u32[]{:S(2)}) copy-start(bf16[64,16,1024]{2,1,0:T(8,128)(2,1)} %param.16) | copy-start | bytes 6291460
  12.6 20.2 %all-to-all-start = ((s32[32,2,1]{1,2,0:T(1,128)}), s32[32,2,1]{1,2,0:T(1,128)S(1)}, u32[]{:S(2)}, u32[]{:S(2)}) async-start(s32[32,2,1]{1,2,0:T(1,128)} %bitcast.1), calls=%async_computation | async-start | bytes 32768 | tf_op jit(solution)/shard_map/all_to_all | solution.py:64
  32.7 13.6 %all-to-all-start.1 = ((s32[32,2,1]{1,2,0:T(1,128)}), s32[32,2,1]{1,2,0:T(1,128)S(1)}, u32[]{:S(2)}, u32[]{:S(2)}) async-start(s32[32,2,1]{1,2,0:T(1,128)} %bitcast.4), calls=%async_computation.1 | async-start | bytes 32768 | tf_op jit(solution)/shard_map/all_to_all | solution.py:67
  40.9 11.2 %copy-start.12 = (bf16[5,512]{1,0:T(8,128)(2,1)S(1)}, bf16[5,512]{1,0:T(8,128)(2,1)}, u32[]{:S(2)}) copy-start(bf16[5,512]{1,0:T(8,128)(2,1)} %param.12) | copy-start | bytes 15364
  40.9 97.6 %copy-start.10 = (bf16[512,32]{0,1:T(8,128)(2,1)S(1)}, bf16[512,32]{0,1:T(8,128)(2,1)}, u32[]{:S(2)}) copy-start(bf16[512,32]{0,1:T(8,128)(2,1)} %param.14) | copy-start | bytes 98308
  40.9 97.8 %copy-start.18 = (u32[256]{0:T(256)S(1)}, u32[256]{0:T(256)}, u32[]{:S(2)}) copy-start(u32[256]{0:T(256)} %constant.105) | copy-start | bytes 3076
  40.9 99.0 %copy-start.16 = (bf16[512,128]{1,0:T(8,128)(2,1)S(1)}, bf16[512,128]{1,0:T(8,128)(2,1)}, u32[]{:S(2)}) copy-start(bf16[512,128]{1,0:T(8,128)(2,1)} %param.13) | copy-start | bytes 393220
  40.9 140.8 %copy-start.2 = (s32[32]{0:T(128)S(1)}, s32[32]{0:T(128)}, u32[]{:S(2)}) copy-start(s32[32]{0:T(128)} %param.19) | copy-start | bytes 388
  46.3 207.1 %all-to-all-start.2 = ((bf16[64,16,1024]{2,1,0:T(8,128)(2,1)}), bf16[64,16,1024]{2,1,0:T(8,128)(2,1)}, u32[]{:S(2)}, u32[]{:S(2)}) async-start(bf16[64,16,1024]{2,1,0:T(8,128)(2,1)} %broadcast_select_fusion.1), calls=%async_computation.2 | async-start | bytes 4194304 | tf_op jit(solution)/shard_map/all_to_all | solution.py:61
  52.0 197.5 %all-gather.5.cloned.1.call-start = ((), (), s32[]{:S(2)}) async-start(), calls=%async_computation.4 | async-start | bytes 1351680 | tf_op jit(solution)/shard_map/all_gather | solution.py:48
  165.3 84.1 %copy-start.8 = (bf16[20,160]{0,1:T(8,128)(2,1)}, bf16[20,160]{0,1:T(8,128)(2,1)S(1)}, u32[]{:S(2)}) copy-start(bf16[20,160]{0,1:T(8,128)(2,1)S(1)} %dynamic-slice_convert_fusion) | copy-start | bytes 19204
  178.9 398.4 %reduce-scatter.4.cloned.1.call-start = ((), (), s32[]{:S(2)}) async-start(), calls=%async_computation.5 | async-start | bytes 1474560 | tf_op jit(solution)/shard_map/reduce_scatter | solution.py:139
  180.8 201.5 %copy-start.11 = (s32[64]{0:T(128)}, s32[64]{0:T(128)S(1)}, u32[]{:S(2)}) copy-start(s32[64]{0:T(128)S(1)} %eq.48) | copy-start | bytes 772
  181.7 71.8 %copy-start.15 = (s32[64]{0:T(128)}, s32[64]{0:T(128)S(1)}, u32[]{:S(2)}) copy-start(s32[64]{0:T(128)S(1)} %all_to_all.21) | copy-start | bytes 772
  182.5 96.2 %copy-start.13 = (pred[64]{0:T(512)(128)(4,1)}, pred[64]{0:T(512)(128)(4,1)S(1)}, u32[]{:S(2)}) copy-start(pred[64]{0:T(512)(128)(4,1)S(1)} %get-tuple-element.22) | copy-start | bytes 196
  257.9 3.7 copy-start.6
  267.5 0.8 copy-start.4
  270.6 8.0 %copy-start.7 = (f32[64,4,8,5]{0,3,2,1:T(8,128)S(1)}, f32[64,4,8,5]{0,3,2,1:T(8,128)}, u32[]{:S(2)}) copy-start(f32[64,4,8,5]{0,3,2,1:T(8,128)} %copy.137) | copy-start | bytes 122884
  276.8 2.6 copy-start.5
  278.7 76.2 %copy-start.14 = (pred[64]{0:T(512)(128)(4,1)S(1)}, pred[64]{0:T(512)(128)(4,1)}, u32[]{:S(2)}) copy-start(pred[64]{0:T(512)(128)(4,1)} %copy-done.13) | copy-start | bytes 196
  397.5 1.7 copy-start.3
  401.8 62.0 %copy-start.17 = (s32[32]{0:T(128)S(1)}, s32[32]{0:T(128)}, u32[]{:S(2)}) copy-start(s32[32]{0:T(128)} %param.21) | copy-start | bytes 388
  401.8 314.4 %all-reduce.5.cloned.1.call-start = ((), (), s32[]{:S(2)}) async-start(), calls=%async_computation.6 | async-start | bytes 327680 | tf_op jit(solution)/shard_map/psum | solution.py:147
  479.1 238.9 %copy-start.9 = (bf16[512,128]{1,0:T(8,128)(2,1)S(1)}, bf16[512,128]{1,0:T(8,128)(2,1)}, u32[]{:S(2)}) copy-start(bf16[512,128]{1,0:T(8,128)(2,1)} %param.15) | copy-start | bytes 393220
  716.2 29.8 %copy-start.1 = (bf16[64,16,1024]{2,1,0:T(8,128)(2,1)S(1)}, bf16[64,16,1024]{2,1,0:T(8,128)(2,1)}, u32[]{:S(2)}) copy-start(bf16[64,16,1024]{2,1,0:T(8,128)(2,1)} %param.16) | copy-start | bytes 6291460
Sparse Core Ops, SparseCore 0:
  179.0 70.3 all-gather.4
  401.9 30.6 reduce-scatter.3
  579.1 137.0 all-reduce.4
where the time goes:
time: 758 us; the launch traced here: 753 us
  blocking collectives  379 us (50%)
  waiting for transfers between devices  215 us (28%)
  local copies, waits for them, and re-layouts  74.7 us (10%)
  matrix products  24.9 us (3%)
  starting transfers between devices  22.9 us (3%)
  other arithmetic  20.5 us (3%)
  between operations  15.9 us (2%)
    psum x1, waiting for transfers between devices, on_device(): lax.psum(part_sums.astype(jnp.bfloat16), 'wide').astype(jnp.float32)  137 us
    all_gather x1, blocking collectives, on_device(): rows_all = lax.all_gather(hidden, 'wide', axis=0, tiled=True)  86.4 us
    pmax x1, blocking collectives, on_device(): peak_all = lax.pmax(state[0], ('wide', 'narrow'))  75.1 us
    unnamed x3, blocking collectives  73 us
    psum x1, blocking collectives, on_device(): lax.psum(part_totals.astype(jnp.bfloat16), 'wide').astype(jnp.float32)  72.1 us
    all_gather x1, waiting for transfers between devices, on_device(): lax.all_gather(query_rows, 'wide', axis=1, tiled=True)  66.8 us
    all_gather x1, blocking collectives, on_device(): lax.all_gather(keyval_rows, 'wide', axis=1, tiled=True)  47 us
  transfers between devices with their start and end apart: 6, of which 4 were waited for; matrix products, arithmetic and copies ran while one was open for 4% of the time, Pallas kernels for 0%

commit v1 on v0

--- a/solution.py
+++ b/solution.py
@@ -10,6 +10,10 @@
 STEPS = 5
 PAGE = 16
 NEG_FILL = -1e30
+
+
+def guide_pipes(in_array):
+    return jnp.sum(lax.all_gather(in_array, axis_name="wide"), axis=0)
 
 
 def combine(first, second):
@@ -145,7 +149,7 @@
     )
     full_sums, full_totals = (
         lax.psum(part_sums.astype(jnp.bfloat16), "wide").astype(jnp.float32),
-        lax.psum(part_totals.astype(jnp.bfloat16), "wide").astype(jnp.float32),
+        guide_pipes(part_totals.astype(jnp.bfloat16)).astype(jnp.float32),
     )
     block_peaks = lax.dynamic_slice_in_dim(peak_all, first_head, head_count, 1)
     final = combine(

time: 758 us -> 734 us (0.968)
  blocking collectives: 379 us -> 355 us
    psum x1 -> x0, blocking collectives: 72.1 us -> none  [on_device(): lax.psum(part_totals.astype(jnp.bfloat16), 'wide').astype(jnp.float32)]
    all_gather x0 -> x1, blocking collectives: none -> 48.1 us  [guide_pipes(): return jnp.sum(lax.all_gather(in_array, axis_name='wide'), axis=0)]
  transfers between devices with their start and end apart: 6 -> 6, of which waited for: 4 -> 4; matrix products, arithmetic and copies ran while one was open for 4% -> 5% of each run, Pallas kernels for 0% -> 0%
where the time goes in v1:
time: 734 us; the launch traced here: 729 us
  blocking collectives  355 us (48%)
  waiting for transfers between devices  215 us (29%)
  local copies, waits for them, and re-layouts  74.7 us (10%)
  matrix products  24.9 us (3%)
  starting transfers between devices  22.9 us (3%)
  other arithmetic  20.5 us (3%)
  between operations  15.9 us (2%)
    psum x1, waiting for transfers between devices, on_device(): lax.psum(part_sums.astype(jnp.bfloat16), 'wide').astype(jnp.float32)  137 us
    all_gather x1, blocking collectives, on_device(): rows_all = lax.all_gather(hidden, 'wide', axis=0, tiled=True)  86.4 us
    pmax x1, blocking collectives, on_device(): peak_all = lax.pmax(state[0], ('wide', 'narrow'))  75.1 us
    unnamed x3, blocking collectives  73 us
    all_gather x1, waiting for transfers between devices, on_device(): lax.all_gather(query_rows, 'wide', axis=1, tiled=True)  66.8 us
    all_gather x1, blocking collectives, guide_pipes(): return jnp.sum(lax.all_gather(in_array, axis_name='wide'), axis=0)  48.1 us
    all_gather x1, blocking collectives, on_device(): lax.all_gather(keyval_rows, 'wide', axis=1, tiled=True)  47 us
  transfers between devices with their start and end apart: 6, of which 4 were waited for; matrix products, arithmetic and copies ran while one was open for 5% of the time, Pallas kernels for 0%

profile of v1, /device:TPU:8, one launch (start us, length us, event | category | flops | bytes accessed | tf_op | source)
XLA Modules:
  0.0 728.6 jit_solution(4761783721595958750)
XLA Ops:
  7.2 1.0 convert_reduce_fusion
  8.2 0.7 multiply_add_fusion.1
  9.0 1.4 gather_fusion.5
  10.4 1.4 gather_fusion.4
  11.9 0.7 all_to_all.17
  12.6 11.7 %all-to-all-start = ((s32[32,2,1]{1,2,0:T(1,128)}), s32[32,2,1]{1,2,0:T(1,128)S(1)}, u32[]{:S(2)}, u32[]{:S(2)}) async-start(s32[32,2,1]{1,2,0:T(1,128)} %bitcast.1), calls=%async_computation | async-start | bytes 32768 | tf_op jit(solution)/shard_map/all_to_all | solution.py:68
  24.3 0.7 all_to_all.19
  25.0 2.0 gather_fusion.1
  27.0 5.7 all-to-all-done
  32.7 5.0 all-to-all-start.1
  37.7 3.2 broadcast_select_fusion.1
  40.9 5.4 all-to-all-done.1
  46.3 5.6 all-to-all-start.2
  52.0 86.4 %all-gather.1 = bf16[32,5,512]{2,1,0:T(8,128)(2,1)S(1)} all-gather(bf16[1,5,512]{2,1,0:T(8,128)(2,1)S(1)} %bitcast.135), channel_id=1, replica_groups=mesh['wide'=32,'narrow'=8] {'wide'}, dimensions={0}, use_global_device_ids=true | all-gather | bytes 168960 | tf_op jit(solution)/shard_map/all_gather | solution.py:35
  140.1 25.1 %all-reduce = bf16[160,160]{0,1:T(8,128)(2,1)S(1)} all-reduce(f32[160,160]{0,1:T(8,128)S(1)} %convolution_bitcast_fusion.1), channel_id=3, replica_groups=mesh['wide'=32,'narrow'=8] {'narrow'}, use_global_device_ids=true, to_apply=%region_2.0.clone | all-reduce | flops 25600 | bytes 153600
  165.4 12.8 %all-gather.2 = bf16[8,20,128]{2,1,0:T(8,128)(2,1)S(1)} all-gather(bf16[1,20,128]{2,1,0:T(8,128)(2,1)S(1)} %copy.158), channel_id=1, replica_groups=mesh['wide'=32,'narrow'=8] {'narrow'}, dimensions={0}, use_global_device_ids=true | all-gather | bytes 46080 | tf_op jit(solution)/shard_map/all_gather | solution.py:48
  178.3 0.6 reshape.291
  179.9 0.7 fusion.47
  180.9 0.7 reduce.13
  181.7 0.8 gather_fusion
  182.6 66.8 %all-gather.7.cloned.1.call-done = bf16[160,4096]{1,0:T(8,128)(2,1)} async-done(((bf16[160,128]{1,0:T(8,128)(2,1)}), bf16[160,4096]{1,0:T(8,128)(2,1)}) %all-gather.7.cloned.1.call-update) | async-done | bytes 1310736 | tf_op jit(solution)/shard_map/all_gather | solution.py:52
  249.5 1.6 copy.221
  251.1 2.4 gather_fusion.2
  253.4 4.4 reshape.221
  257.9 3.7 fusion.50
  261.5 3.5 bitcast_reduce_fusion
  265.5 1.2 copy.189
  266.7 0.7 select_reduce_fusion
  267.5 0.8 copy-done.4
  268.4 1.0 gather_fusion.3
  269.7 0.9 copy.163
  270.6 6.2 fusion.4
  276.8 1.8 copy.188
  279.7 75.1 %pmax.7 = f32[160,32]{0,1:T(8,128)S(1)} all-reduce(f32[160,32]{0,1:T(8,128)S(1)} %copy.171), channel_id=1, replica_groups=mesh['wide'=32,'narrow'=8] {'wide','narrow'}, use_global_device_ids=true, to_apply=%region_5.7 | all-reduce | flops 5120 | bytes 40960 | tf_op jit(solution)/shard_map/pmax | solution.py:139
  354.9 0.9 subtract_exponential_fusion
  355.9 1.8 copy.165
  357.6 5.5 broadcast_multiply_fusion
  363.1 5.1 copy.166
  368.2 6.7 reshape.223
  374.9 7.3 %dot_general.39 = f32[4,8,5,128,64]{3,2,1,0,4:T(8,128)} reshape(f32[20480,64]{0,1:T(8,128)} %bitcast.125) | data formatting | bytes 10485760 | tf_op jit(solution)/shard_map/dot_general | solution.py:107
  382.3 8.2 %fusion.17 = f32[32,5,4,8,128]{4,0,1,3,2:T(8,128)S(1)} fusion(f32[4,8,5,128,64]{3,2,1,0,4:T(8,128)} %dot_general.39, s32[64]{0:T(128)S(1)} %eq.48), kind=kOutput, calls=%fused_computation.30 | convolution fusion | flops 503318528 | bytes 7864576 | tf_op jit(solution)/shard_map/dot_general | solution.py:107
  390.5 3.0 copy.168
  393.5 4.0 reshape.224
  397.5 0.7 mul.96
  398.2 1.0 copy-done.3
  399.2 2.6 fusion.8
  401.9 0.7 slice_bitcast_fusion.1
  402.7 12.8 %all-gather.3 = bf16[8,20,32]{2,1,0:T(8,128)(2,1)S(1)} all-gather(bf16[1,20,32]{2,1,0:T(8,128)(2,1)S(1)} %copy.173), channel_id=1, replica_groups=mesh['wide'=32,'narrow'=8] {'narrow'}, dimensions={0}, use_global_device_ids=true | all-gather | bytes 11520 | tf_op jit(solution)/shard_map/all_gather | solution.py:49
  415.6 47.0 %all_gather.25 = bf16[160,1024]{0,1:T(8,128)(2,1)S(1)} all-gather(bf16[160,32]{0,1:T(8,128)(2,1)S(1)} %copy.207), channel_id=1, replica_groups=mesh['wide'=32,'narrow'=8] {'wide'}, dimensions={1}, use_global_device_ids=true | all-gather | bytes 337920 | tf_op jit(solution)/shard_map/all_gather | solution.py:53
  464.3 0.6 iota_compare_fusion.6
  465.0 0.7 dynamic-slice_select_fusion
  465.8 6.4 fusion.20
  472.2 2.5 copy.178
  476.0 2.3 copy.185
  478.3 0.8 convolution_bitcast_fusion
  479.1 1.8 copy.186
  481.1 23.9 %all-reduce.1 = bf16[160,32]{1,0:T(8,128)(2,1)S(1)} all-reduce(bf16[160,32]{1,0:T(8,128)(2,1)S(1)} %copy.194), channel_id=5, replica_groups=mesh['wide'=32,'narrow'=8] {'narrow'}, use_global_device_ids=true, to_apply=%region_10.12.clone | all-reduce | flops 5120 | bytes 20480
  505.2 48.1 %all-gather.4 = bf16[32,160,4]{1,2,0:T(4,128)(2,1)S(1)} all-gather(bf16[1,160,4]{1,2,0:T(4,128)(2,1)S(1)} %copy.195), channel_id=2, replica_groups=mesh['wide'=32,'narrow'=8] {'wide'}, dimensions={0}, use_global_device_ids=true | all-gather | bytes 42240 | tf_op jit(solution)/shard_map/all_gather | solution.py:16
  553.4 1.6 reshape.226
  555.4 136.7 %all-reduce.5.cloned.1.call-done = bf16[160,4,128]{2,1,0:T(4,128)(2,1)} async-done(((bf16[160,4,128]{2,1,0:T(4,128)(2,1)}), bf16[160,4,128]{2,1,0:T(4,128)(2,1)}) %all-reduce.5.cloned.1.call-update) | async-done | bytes 163856 | tf_op jit(solution)/shard_map/psum | solution.py:151
  692.1 1.8 fusion.25
  694.1 23.9 %all-reduce.2 = bf16[160,128]{1,0:T(8,128)(2,1)S(1)} all-reduce(bf16[160,128]{1,0:T(8,128)(2,1)S(1)} %convolution_convert_fusion), channel_id=6, replica_groups=mesh['wide'=32,'narrow'=8] {'narrow'}, use_global_device_ids=true, to_apply=%region_13.15.clone | all-reduce | flops 20480 | bytes 81920
  718.1 0.6 constant_dynamic-slice_fusion.2
  718.7 3.2 copy.253
  (111 shorter events, 8.7 us)
Async XLA Ops:
  7.2 17.9 %copy-start = (bf16[64,16,1024]{2,1,0:T(8,128)(2,1)S(1)}, bf16[64,16,1024]{2,1,0:T(8,128)(2,1)}, u32[]{:S(2)}) copy-start(bf16[64,16,1024]{2,1,0:T(8,128)(2,1)} %param.16) | copy-start | bytes 6291460
  12.6 20.2 %all-to-all-start = ((s32[32,2,1]{1,2,0:T(1,128)}), s32[32,2,1]{1,2,0:T(1,128)S(1)}, u32[]{:S(2)}, u32[]{:S(2)}) async-start(s32[32,2,1]{1,2,0:T(1,128)} %bitcast.1), calls=%async_computation | async-start | bytes 32768 | tf_op jit(solution)/shard_map/all_to_all | solution.py:68
  32.7 13.6 %all-to-all-start.1 = ((s32[32,2,1]{1,2,0:T(1,128)}), s32[32,2,1]{1,2,0:T(1,128)S(1)}, u32[]{:S(2)}, u32[]{:S(2)}) async-start(s32[32,2,1]{1,2,0:T(1,128)} %bitcast.4), calls=%async_computation.1 | async-start | bytes 32768 | tf_op jit(solution)/shard_map/all_to_all | solution.py:71
  40.9 11.2 %copy-start.12 = (bf16[5,512]{1,0:T(8,128)(2,1)S(1)}, bf16[5,512]{1,0:T(8,128)(2,1)}, u32[]{:S(2)}) copy-start(bf16[5,512]{1,0:T(8,128)(2,1)} %param.12) | copy-start | bytes 15364
  40.9 97.6 %copy-start.10 = (bf16[512,32]{0,1:T(8,128)(2,1)S(1)}, bf16[512,32]{0,1:T(8,128)(2,1)}, u32[]{:S(2)}) copy-start(bf16[512,32]{0,1:T(8,128)(2,1)} %param.14) | copy-start | bytes 98308
  40.9 97.8 %copy-start.18 = (u32[256]{0:T(256)S(1)}, u32[256]{0:T(256)}, u32[]{:S(2)}) copy-start(u32[256]{0:T(256)} %constant.106) | copy-start | bytes 3076
  40.9 99.0 %copy-start.16 = (bf16[512,128]{1,0:T(8,128)(2,1)S(1)}, bf16[512,128]{1,0:T(8,128)(2,1)}, u32[]{:S(2)}) copy-start(bf16[512,128]{1,0:T(8,128)(2,1)} %param.13) | copy-start | bytes 393220
  40.9 140.8 %copy-start.2 = (s32[32]{0:T(128)S(1)}, s32[32]{0:T(128)}, u32[]{:S(2)}) copy-start(s32[32]{0:T(128)} %param.19) | copy-start | bytes 388
  46.3 207.1 %all-to-all-start.2 = ((bf16[64,16,1024]{2,1,0:T(8,128)(2,1)}), bf16[64,16,1024]{2,1,0:T(8,128)(2,1)}, u32[]{:S(2)}, u32[]{:S(2)}) async-start(bf16[64,16,1024]{2,1,0:T(8,128)(2,1)} %broadcast_select_fusion.1), calls=%async_computation.2 | async-start | bytes 4194304 | tf_op jit(solution)/shard_map/all_to_all | solution.py:65
  52.0 197.5 %all-gather.7.cloned.1.call-start = ((), (), s32[]{:S(2)}) async-start(), calls=%async_computation.4 | async-start | bytes 1351680 | tf_op jit(solution)/shard_map/all_gather | solution.py:52
  165.3 84.1 %copy-start.8 = (bf16[20,160]{0,1:T(8,128)(2,1)}, bf16[20,160]{0,1:T(8,128)(2,1)S(1)}, u32[]{:S(2)}) copy-start(bf16[20,160]{0,1:T(8,128)(2,1)S(1)} %dynamic-slice_convert_fusion) | copy-start | bytes 19204
  178.9 374.5 %reduce-scatter.4.cloned.1.call-start = ((), (), s32[]{:S(2)}) async-start(), calls=%async_computation.5 | async-start | bytes 1474560 | tf_op jit(solution)/shard_map/reduce_scatter | solution.py:143
  180.8 201.5 %copy-start.11 = (s32[64]{0:T(128)}, s32[64]{0:T(128)S(1)}, u32[]{:S(2)}) copy-start(s32[64]{0:T(128)S(1)} %eq.48) | copy-start | bytes 772
  181.7 71.8 %copy-start.15 = (s32[64]{0:T(128)}, s32[64]{0:T(128)S(1)}, u32[]{:S(2)}) copy-start(s32[64]{0:T(128)S(1)} %all_to_all.21) | copy-start | bytes 772
  182.5 96.2 %copy-start.13 = (pred[64]{0:T(512)(128)(4,1)}, pred[64]{0:T(512)(128)(4,1)S(1)}, u32[]{:S(2)}) copy-start(pred[64]{0:T(512)(128)(4,1)S(1)} %get-tuple-element.22) | copy-start | bytes 196
  257.9 3.7 copy-start.6
  267.5 0.8 copy-start.4
  270.6 8.0 %copy-start.7 = (f32[64,4,8,5]{0,3,2,1:T(8,128)S(1)}, f32[64,4,8,5]{0,3,2,1:T(8,128)}, u32[]{:S(2)}) copy-start(f32[64,4,8,5]{0,3,2,1:T(8,128)} %copy.189) | copy-start | bytes 122884
  276.8 2.6 copy-start.5
  278.7 76.2 %copy-start.14 = (pred[64]{0:T(512)(128)(4,1)S(1)}, pred[64]{0:T(512)(128)(4,1)}, u32[]{:S(2)}) copy-start(pred[64]{0:T(512)(128)(4,1)} %copy-done.13) | copy-start | bytes 196
  397.5 1.7 copy-start.3
  401.8 62.0 %copy-start.17 = (s32[32]{0:T(128)S(1)}, s32[32]{0:T(128)}, u32[]{:S(2)}) copy-start(s32[32]{0:T(128)} %param.21) | copy-start | bytes 388
  401.8 290.3 %all-reduce.5.cloned.1.call-start = ((), (), s32[]{:S(2)}) async-start(), calls=%async_computation.6 | async-start | bytes 327680 | tf_op jit(solution)/shard_map/psum | solution.py:151
  479.1 214.8 %copy-start.9 = (bf16[512,128]{1,0:T(8,128)(2,1)S(1)}, bf16[512,128]{1,0:T(8,128)(2,1)}, u32[]{:S(2)}) copy-start(bf16[512,128]{1,0:T(8,128)(2,1)} %param.15) | copy-start | bytes 393220
  692.1 29.8 %copy-start.1 = (bf16[64,16,1024]{2,1,0:T(8,128)(2,1)S(1)}, bf16[64,16,1024]{2,1,0:T(8,128)(2,1)}, u32[]{:S(2)}) copy-start(bf16[64,16,1024]{2,1,0:T(8,128)(2,1)} %param.16) | copy-start | bytes 6291460
Sparse Core Ops, SparseCore 0:
  179.0 70.3 all-gather.6
  401.9 30.6 reduce-scatter.3
  555.1 136.8 all-reduce.4
